TPU v7x, 32 devices: a whole 2x2x4 slice. The times are simulated.
32 devices in a mesh: groups: 2 (over y), shard: 4 (over z), sub: 2 (over x), chan: 2 (over core).
Axes of the slice: x: 2, y: 2, z: 4, core: 2. Of those that a mesh axis runs over, the one named last changes fastest.
Arguments:
- field: bfloat16 [32, 8, 96, 128], P(('groups', 'shard'), 'sub', 'chan'), parts along dimension 0, may hold values from -6 to 6
- cotangent: bfloat16 [32, 8, 96, 128], P(('groups', 'shard'), 'sub', 'chan'), parts along dimension 0, may hold values from -6 to 6
- space_weight: bfloat16 [3, 3, 96, 96], replicated, may hold values from -0.21875 to 0.21875
- time_weight: bfloat16 [9, 96], P(None, 'chan'), may hold values from -2 to 2
Outputs:
- output: bfloat16 [32, 8, 96, 128], P(('groups', 'shard'), 'sub', 'chan'), parts along dimension 0
- field_grad: bfloat16 [32, 8, 96, 128], P(('groups', 'shard'), 'sub', 'chan'), parts along dimension 0
- space_grad: float32 [6, 3, 96, 96], P('groups', None, 'chan'), parts along dimension 0
- time_grad: float32 [18, 96], P('groups', 'chan'), parts along dimension 0
There are 2 independent parts, one for each index of `groups`. A program takes and returns all parts, laid end to end along the dimension named above; an argument that names none is the same for every part. Nothing has to cross between parts.
All inputs are finite; a program needn't handle non-finite values.
Results may differ from a plain program's by a relative error of at most 0.0048.
Values may be sent and summed in bfloat16 or wider, within the bound.
A program may use at most 64 MiB of HBM per device.

v0:
```python
import jax
import jax.numpy as jnp
from jax import lax
from jax.sharding import PartitionSpec as P


def with_halo(cells, sides, width):
    for axis, dim in sides:
        count = lax.axis_size(axis)
        ends = count - 1
        head = lax.slice_in_dim(cells, 0, width, axis=dim)
        tail = lax.slice_in_dim(cells, cells.shape[dim] - width, cells.shape[dim], axis=dim)
        cells = jnp.concatenate(
            [
                lax.ppermute(tail, axis, [(i, (i + 1) % count) for i in range(ends)]),
                cells,
                lax.ppermute(head, axis, [((i + 1) % count, i) for i in range(ends)]),
            ],
            axis=dim,
        )
    return cells


def gelu_tanh(values):
    return jax.nn.gelu(values, approximate=True)


def widen(values):
    rimmed = with_halo(values, (("sub", 1),), 1)
    gathered = lax.all_gather(rimmed, "chan", axis=2, tiled=True)
    return jnp.pad(gathered, ((0, 0), (0, 0), (0, 0), (1, 1)))


def to_time(values):
    return lax.all_to_all(values, "shard", split_axis=1, concat_axis=0, tiled=True)


def to_space(values):
    return lax.all_to_all(values, "shard", split_axis=0, concat_axis=1, tiled=True)


def pad_time(values):
    return jnp.pad(values, ((4, 4), (0, 0), (0, 0), (0, 0)))


def time_forward(padded, taps, count):
    total = jnp.zeros((count,) + padded.shape[1:], jnp.float32)
    for k in range(9):
        total = total + taps[k][:, None] * padded[k : k + count]
    return total


def time_back(padded, taps, count):
    total = jnp.zeros((count,) + padded.shape[1:], jnp.float32)
    for k in range(9):
        total = total + taps[k][:, None] * padded[8 - k : 8 - k + count]
    return total


def time_weight_part(grads, padded, count):
    grads32 = grads.astype(jnp.float32)
    parts = []
    for k in range(9):
        parts.append(jnp.sum(grads32 * padded[k : k + count], axis=(0, 1, 3)))
    return jnp.stack(parts)


def on_device(field, cotangent, space_weight, time_weight):
    frames_here, rows, width_own, cells = field.shape
    start = lax.axis_index("chan") * width_own
    tap_rows = lax.dynamic_slice_in_dim(space_weight, start, width_own, 2)
    tap_cols = lax.dynamic_slice_in_dim(space_weight, start, width_own, 3)
    taps = time_weight.astype(jnp.float32)
    full = widen(field)
    hidden = jnp.zeros(field.shape, jnp.float32)
    for i in range(3):
        for j in range(3):
            hidden = hidden + jnp.einsum(
                "oc,frcw->frow",
                tap_rows[i, j],
                full[:, i : i + rows, :, j : j + cells],
                preferred_element_type=jnp.float32,
            )
    act, pull = jax.vjp(gelu_tanh, hidden)
    acts = act.astype(jnp.bfloat16)
    acts_time = to_time(acts)
    acts_pad = pad_time(acts_time)
    frames = acts_time.shape[0]
    mixed = to_space(time_forward(acts_pad, taps, frames).astype(jnp.bfloat16))
    grad_time = to_time(cotangent)
    back_local = time_back(pad_time(grad_time), taps, frames).astype(jnp.bfloat16)
    time_part = time_weight_part(grad_time, acts_pad, frames)
    back_time = to_space(back_local)
    output = (field.astype(jnp.float32) + mixed.astype(jnp.float32)).astype(jnp.bfloat16)
    back_hidden = pull(back_time.astype(jnp.float32))[0].astype(jnp.bfloat16)
    wide_grad = widen(back_hidden)
    back_field = cotangent.astype(jnp.float32)
    space_rows = []
    for i in range(3):
        inner = []
        for j in range(3):
            back_field = back_field + jnp.einsum(
                "oc,frow->frcw",
                tap_cols[i, j],
                wide_grad[:, 2 - i : 2 - i + rows, :, 2 - j : 2 - j + cells],
                preferred_element_type=jnp.float32,
            )
            inner.append(
                jnp.einsum(
                    "frow,frcw->oc",
                    back_hidden,
                    full[:, i : i + rows, :, j : j + cells],
                    preferred_element_type=jnp.float32,
                )
            )
        space_rows.append(jnp.stack(inner))
    field_grad = back_field.astype(jnp.bfloat16)
    space_part = jnp.stack(space_rows)
    space_total, time_total = lax.psum((space_part, time_part), ("shard", "sub"))
    total_frames = frames_here * lax.axis_size("shard")
    total_rows = rows * lax.axis_size("sub")
    scale = float(total_frames * total_rows * cells) ** (-0.5)
    return (output, field_grad, space_total * scale, time_total * scale)


def solution(mesh):
    placed = (
        P(("groups", "shard"), "sub", "chan", None),
        P(("groups", "shard"), "sub", "chan", None),
        P(),
        P(None, "chan"),
    )
    return jax.shard_map(
        on_device,
        mesh=mesh,
        in_specs=placed,
        out_specs=(
            P(("groups", "shard"), "sub", "chan", None),
            P(("groups", "shard"), "sub", "chan", None),
            P("groups", None, "chan", None),
            P("groups", "chan"),
        ),
        check_vma=False,
    )
```

profile of v0, /device:TPU:0, one launch (start us, length us, event | category | flops | bytes accessed | tf_op | source)
XLA Modules:
  0.0 162.7 jit_solution(8335515254754302777)
XLA Ops:
  7.2 0.9 fusion.95
  8.1 4.9 %collective-permute-start = (bf16[4,1,48,128]{3,2,1,0:T(8,128)(2,1)S(1)}, bf16[4,1,48,128]{3,2,1,0:T(8,128)(2,1)S(1)}, u32[]{:S(2)}, u32[]{:S(2)}) collective-permute-start(bf16[4,1,48,128]{3,2,1,0:T(8,128)(2,1)S(1)} %get-tuple-element.24), channel_id=1, source_target_pairs={{0,2},{1,3},{4,6},{5,7},{8,10},{9,11},{12,14},{13,15},{16,18},{17,... | collective-permute-start | bytes 147464 | tf_op jit(solution)/shard_map/ppermute | solution.py:15
  13.0 1.3 collective-permute-start.1
  14.3 1.6 copy.19
  15.9 4.9 %all-to-all-start.2 = ((bf16[4,4,48,128]{3,2,0,1:T(8,128)(2,1)}), bf16[4,4,48,128]{3,2,0,1:T(8,128)(2,1)S(1)}, u32[]{:S(2)}, u32[]{:S(2)}) async-start(bf16[4,4,48,128]{3,2,0,1:T(8,128)(2,1)} %copy.19), calls=%async_computation.2 | async-start | bytes 393216 | tf_op jit(solution)/shard_map/all_to_all | solution.py:35
  20.9 2.2 %all_gather.6 = bf16[4,6,96,128]{3,2,1,0:T(8,128)(2,1)S(1)} all-gather(bf16[4,6,48,128]{3,2,1,0:T(8,128)(2,1)S(1)} %pad_maximum_fusion), channel_id=1, replica_groups=mesh['groups'=2,'shard'=4,'sub'=2,'chan'=2] {'chan'}, dimensions={2}, use_global_device_ids=true | all-gather | bytes 884736 | tf_op jit(solution)/shard_map/all_gather | solution.py:30
  23.1 0.3 fusion.55
  23.6 0.3 convolution_add_fusion.6
  23.9 0.3 convolution_add_fusion.5
  24.5 0.3 convolution_add_fusion.3
  24.8 3.2 %all-to-all-done.2 = bf16[4,4,48,128]{3,2,0,1:T(8,128)(2,1)S(1)} async-done(((bf16[4,4,48,128]{3,2,0,1:T(8,128)(2,1)}), bf16[4,4,48,128]{3,2,0,1:T(8,128)(2,1)S(1)}, u32[]{:S(2)}, u32[]{:S(2)}) %all-to-all-start.2) | async-done | bytes 196640 | tf_op jit(solution)/shard_map/all_to_all | solution.py:35
  28.1 1.0 fusion.56
  29.1 3.4 %all-to-all-start.3 = ((bf16[16,1,48,128]{3,2,1,0:T(8,128)(2,1)}), bf16[16,1,48,128]{3,2,1,0:T(8,128)(2,1)S(1)}, u32[]{:S(2)}, u32[]{:S(2)}) async-start(bf16[16,1,48,128]{3,2,1,0:T(8,128)(2,1)} %fusion.56), calls=%async_computation.3 | async-start | bytes 393216 | tf_op jit(solution)/shard_map/all_to_all | solution.py:39
  32.4 0.3 convolution_add_fusion.2
  33.0 5.7 %all-to-all-done.3 = bf16[16,1,48,128]{3,2,1,0:T(8,128)(2,1)S(1)} async-done(((bf16[16,1,48,128]{3,2,1,0:T(8,128)(2,1)}), bf16[16,1,48,128]{3,2,1,0:T(8,128)(2,1)S(1)}, u32[]{:S(2)}, u32[]{:S(2)}) %all-to-all-start.3) | async-done | bytes 196640 | tf_op jit(solution)/shard_map/all_to_all | solution.py:39
  38.7 0.6 fusion.26
  39.5 0.3 convolution_bitcast_fusion.11
  39.8 0.3 convolution_bitcast_fusion.12
  40.1 0.2 convolution_bitcast_fusion.13
  40.4 0.3 convolution_bitcast_fusion.14
  40.7 0.3 convolution_bitcast_fusion.15
  41.1 0.2 convolution_bitcast_fusion.16
  41.3 0.3 convolution_bitcast_fusion.17
  41.7 0.3 convolution_bitcast_fusion.9
  42.0 0.7 copy.16
  42.7 3.4 %all-to-all-start = ((bf16[4,4,48,128]{3,2,0,1:T(8,128)(2,1)}), bf16[4,4,48,128]{3,2,0,1:T(8,128)(2,1)S(1)}, u32[]{:S(2)}, u32[]{:S(2)}) async-start(bf16[4,4,48,128]{3,2,0,1:T(8,128)(2,1)} %copy.16), calls=%async_computation | async-start | bytes 393216 | tf_op jit(solution)/shard_map/all_to_all | solution.py:35
  46.1 4.5 %collective-permute-start.2 = (bf16[4,1,48,128]{3,2,1,0:T(8,128)(2,1)S(1)}, bf16[4,1,48,128]{3,2,1,0:T(8,128)(2,1)S(1)}, u32[]{:S(2)}, u32[]{:S(2)}) collective-permute-start(bf16[4,1,48,128]{3,2,1,0:T(8,128)(2,1)S(1)} %get-tuple-element.22), channel_id=1, source_target_pairs={{0,2},{1,3},{4,6},{5,7},{8,10},{9,11},{12,14},{13,15},{16,18},{17,... | collective-permute-start | bytes 147464 | tf_op jit(solution)/shard_map/ppermute | solution.py:15
  50.7 1.3 collective-permute-start.3
  52.0 0.7 pad_maximum_fusion.2
  52.8 3.9 %collective-permute-done.3 = bf16[4,1,48,128]{3,2,1,0:T(8,128)(2,1)S(1)} collective-permute-done((bf16[4,1,48,128]{3,2,1,0:T(8,128)(2,1)S(1)}, bf16[4,1,48,128]{3,2,1,0:T(8,128)(2,1)S(1)}, u32[]{:S(2)}, u32[]{:S(2)}) %collective-permute-start.3) | collective-permute-done | bytes 49184 | tf_op jit(solution)/shard_map/ppermute | solution.py:17
  56.7 2.4 %all_gather.7 = bf16[4,6,96,128]{3,2,1,0:T(8,128)(2,1)S(1)} all-gather(bf16[4,6,48,128]{3,2,1,0:T(8,128)(2,1)S(1)} %pad_maximum_fusion.1), channel_id=1, replica_groups=mesh['groups'=2,'shard'=4,'sub'=2,'chan'=2] {'chan'}, dimensions={2}, use_global_device_ids=true | all-gather | bytes 884736 | tf_op jit(solution)/shard_map/all_gather | solution.py:30
  59.1 0.3 fusion.8
  59.4 0.3 fusion.7
  59.7 0.3 fusion.6
  60.1 0.3 fusion.5
  60.4 0.3 fusion.4
  60.8 0.3 fusion.3
  61.1 0.3 fusion.2
  61.5 0.3 fusion.1
  61.8 1.0 fusion.10
  62.8 63.5 %all-reduce.6.cloned.1.call-done = f32[3,3,48,96]{3,2,1,0:T(8,128)} async-done(((f32[3,3,48,96]{3,2,1,0:T(8,128)}), f32[3,3,48,96]{3,2,1,0:T(8,128)}) %all-reduce.6.cloned.1.call-update) | async-done | bytes 165904 | tf_op jit(solution)/shard_map/psum | solution.py:119
  126.3 1.6 %broadcast_multiply_fusion = f32[3,3,48,96]{3,2,1,0:T(8,128)} fusion(f32[3,3,48,96]{3,2,1,0:T(8,128)} %all-reduce.6.cloned.1.call-done), kind=kLoop, calls=%fused_computation.138 | loop fusion | flops 41472 | bytes 331776 | tf_op jit(solution)/shard_map/mul | solution.py:123
  128.0 1.0 fusion.57
  129.0 0.4 fusion.40
  129.4 3.7 %all-to-all-start.1 = ((bf16[16,1,48,128]{3,2,1,0:T(8,128)(2,1)}), bf16[16,1,48,128]{3,2,1,0:T(8,128)(2,1)S(1)}, u32[]{:S(2)}, u32[]{:S(2)}) async-start(bf16[16,1,48,128]{3,2,1,0:T(8,128)(2,1)} %fusion.57), calls=%async_computation.1 | async-start | bytes 393216 | tf_op jit(solution)/shard_map/all_to_all | solution.py:39
  133.2 21.3 %psum.15 = f32[9,48]{1,0:T(8,128)S(1)} all-reduce(f32[9,48]{1,0:T(8,128)S(1)} %stack.103), channel_id=1, replica_groups=mesh['groups'=2,'shard'=4,'sub'=2,'chan'=2] {'shard','sub'}, use_global_device_ids=true, to_apply=%region_10.11 | all-reduce | flops 432 | bytes 3456 | tf_op jit(solution)/shard_map/psum | solution.py:119
  154.5 0.6 broadcast_multiply_fusion.1
  155.2 0.7 copy.24
  (29 shorter events, 1.3 us)
Async XLA Ops:
  7.2 15.9 %copy-start = (bf16[3,3,96,96]{3,2,1,0:T(8,128)(2,1)S(1)}, bf16[3,3,96,96]{3,2,1,0:T(8,128)(2,1)}, u32[]{:S(2)}) copy-start(bf16[3,3,96,96]{3,2,1,0:T(8,128)(2,1)} %param.6) | copy-start | bytes 497668
  7.2 13.6 %copy-start.1 = (bf16[4,4,48,128]{3,2,1,0:T(8,128)(2,1)S(1)}, bf16[4,4,48,128]{3,2,1,0:T(8,128)(2,1)}, u32[]{:S(2)}) copy-start(bf16[4,4,48,128]{3,2,1,0:T(8,128)(2,1)} %param.4) | copy-start | bytes 589828
  7.2 13.6 %copy-start.3 = (bf16[9,48]{1,0:T(8,128)(2,1)S(1)}, bf16[9,48]{1,0:T(8,128)(2,1)}, u32[]{:S(2)}) copy-start(bf16[9,48]{1,0:T(8,128)(2,1)} %param.7) | copy-start | bytes 2596
  8.1 12.7 %collective-permute-start = (bf16[4,1,48,128]{3,2,1,0:T(8,128)(2,1)S(1)}, bf16[4,1,48,128]{3,2,1,0:T(8,128)(2,1)S(1)}, u32[]{:S(2)}, u32[]{:S(2)}) collective-permute-start(bf16[4,1,48,128]{3,2,1,0:T(8,128)(2,1)S(1)} %get-tuple-element.24), channel_id=1, source_target_pairs={{0,2},{1,3},{4,6},{5,7},{8,10},{9,11},{12,14},{13,15},{16,18},{17,... | collective-permute-start | bytes 147464 | tf_op jit(solution)/shard_map/ppermute | solution.py:15
  13.0 7.8 %collective-permute-start.1 = (bf16[4,1,48,128]{3,2,1,0:T(8,128)(2,1)S(1)}, bf16[4,1,48,128]{3,2,1,0:T(8,128)(2,1)S(1)}, u32[]{:S(2)}, u32[]{:S(2)}) collective-permute-start(bf16[4,1,48,128]{3,2,1,0:T(8,128)(2,1)S(1)} %get-tuple-element.25), channel_id=1, source_target_pairs={{2,0},{3,1},{6,4},{7,5},{10,8},{11,9},{14,12},{15,13},{18,16},{19,... | collective-permute-start | bytes 147464 | tf_op jit(solution)/shard_map/ppermute | solution.py:17
  15.9 12.2 %all-to-all-start.2 = ((bf16[4,4,48,128]{3,2,0,1:T(8,128)(2,1)}), bf16[4,4,48,128]{3,2,0,1:T(8,128)(2,1)S(1)}, u32[]{:S(2)}, u32[]{:S(2)}) async-start(bf16[4,4,48,128]{3,2,0,1:T(8,128)(2,1)} %copy.19), calls=%async_computation.2 | async-start | bytes 393216 | tf_op jit(solution)/shard_map/all_to_all | solution.py:35
  29.1 9.6 %all-to-all-start.3 = ((bf16[16,1,48,128]{3,2,1,0:T(8,128)(2,1)}), bf16[16,1,48,128]{3,2,1,0:T(8,128)(2,1)S(1)}, u32[]{:S(2)}, u32[]{:S(2)}) async-start(bf16[16,1,48,128]{3,2,1,0:T(8,128)(2,1)} %fusion.56), calls=%async_computation.3 | async-start | bytes 393216 | tf_op jit(solution)/shard_map/all_to_all | solution.py:39
  42.7 85.3 %all-to-all-start = ((bf16[4,4,48,128]{3,2,0,1:T(8,128)(2,1)}), bf16[4,4,48,128]{3,2,0,1:T(8,128)(2,1)S(1)}, u32[]{:S(2)}, u32[]{:S(2)}) async-start(bf16[4,4,48,128]{3,2,0,1:T(8,128)(2,1)} %copy.16), calls=%async_computation | async-start | bytes 393216 | tf_op jit(solution)/shard_map/all_to_all | solution.py:35
  46.1 80.3 %all-reduce.6.cloned.1.call-start = ((), (), s32[]{:S(2)}) async-start(), calls=%async_computation.4 | async-start | bytes 442368 | tf_op jit(solution)/shard_map/psum | solution.py:119
  46.1 6.6 %collective-permute-start.2 = (bf16[4,1,48,128]{3,2,1,0:T(8,128)(2,1)S(1)}, bf16[4,1,48,128]{3,2,1,0:T(8,128)(2,1)S(1)}, u32[]{:S(2)}, u32[]{:S(2)}) collective-permute-start(bf16[4,1,48,128]{3,2,1,0:T(8,128)(2,1)S(1)} %get-tuple-element.22), channel_id=1, source_target_pairs={{0,2},{1,3},{4,6},{5,7},{8,10},{9,11},{12,14},{13,15},{16,18},{17,... | collective-permute-start | bytes 147464 | tf_op jit(solution)/shard_map/ppermute | solution.py:15
  50.7 6.0 %collective-permute-start.3 = (bf16[4,1,48,128]{3,2,1,0:T(8,128)(2,1)S(1)}, bf16[4,1,48,128]{3,2,1,0:T(8,128)(2,1)S(1)}, u32[]{:S(2)}, u32[]{:S(2)}) collective-permute-start(bf16[4,1,48,128]{3,2,1,0:T(8,128)(2,1)S(1)} %get-tuple-element.23), channel_id=1, source_target_pairs={{2,0},{3,1},{6,4},{7,5},{10,8},{11,9},{14,12},{15,13},{18,16},{19,... | collective-permute-start | bytes 147464 | tf_op jit(solution)/shard_map/ppermute | solution.py:17
  56.7 2.4 %copy-start.2 = (bf16[4,4,48,128]{3,2,1,0:T(8,128)(2,1)S(1)}, bf16[4,4,48,128]{3,2,1,0:T(8,128)(2,1)}, u32[]{:S(2)}) copy-start(bf16[4,4,48,128]{3,2,1,0:T(8,128)(2,1)} %param.5) | copy-start | bytes 589828
  129.4 25.8 %all-to-all-start.1 = ((bf16[16,1,48,128]{3,2,1,0:T(8,128)(2,1)}), bf16[16,1,48,128]{3,2,1,0:T(8,128)(2,1)S(1)}, u32[]{:S(2)}, u32[]{:S(2)}) async-start(bf16[16,1,48,128]{3,2,1,0:T(8,128)(2,1)} %fusion.57), calls=%async_computation.1 | async-start | bytes 393216 | tf_op jit(solution)/shard_map/all_to_all | solution.py:39
Sparse Core Ops, SparseCore 0:
  52.9 73.4 all-reduce.5
where the time goes:
time: 163 us
  waiting for transfers between devices  76.4 us (47%)
  starting transfers between devices  27.3 us (17%)
  blocking collectives  25.9 us (16%)
  between operations  14.4 us (9%)
  matrix products  9.13 us (6%)
  other arithmetic  5.67 us (3%)
  local copies, waits for them, and re-layouts  3.97 us (2%)
    psum x1, waiting for transfers between devices, on_device(): lax.psum((space_part, time_part), ('shard', 'sub'))  63.5 us
    psum x1, blocking collectives, on_device(): lax.psum((space_part, time_part), ('shard', 'sub'))  21.3 us
    ppermute x2, starting transfers between devices, with_halo(): lax.ppermute(tail, axis, [(i, (i + 1) % count) for i in range(ends)])  9.39 us
    all_to_all x2, starting transfers between devices, to_time(): lax.all_to_all(values, 'shard', split_axis=1, concat_axis=0, tiled=True)  8.24 us
    all_to_all x2, starting transfers between devices, to_space(): lax.all_to_all(values, 'shard', split_axis=0, concat_axis=1, tiled=True)  7.02 us
    all_to_all x2, waiting for transfers between devices, to_space(): lax.all_to_all(values, 'shard', split_axis=0, concat_axis=1, tiled=True)  5.68 us
    all_gather x2, blocking collectives, widen(): gathered = lax.all_gather(rimmed, 'chan', axis=2, tiled=True)  4.59 us
    ppermute x2, waiting for transfers between devices, with_halo(): lax.ppermute(head, axis, [((i + 1) % count, i) for i in range(ends)])  3.9 us
  transfers between devices with their start and end apart: 9, of which 4 were waited for; matrix products, arithmetic and copies ran while one was open for 7% of the time, Pallas kernels for 0%

commit v1 on v0

v1 whole, which is shorter than its diff:
```python
import functools

import jax
import jax.numpy as jnp
from jax import lax
from jax.experimental import pallas as pl
from jax.experimental.pallas import tpu as pltpu
from jax.sharding import PartitionSpec as P

F32 = jnp.float32
BF16 = jnp.bfloat16
WIRE = jnp.float32
ROOT = 0.7978845608028654
CUBE = 0.044715
MESH = pl.DeviceIdType.MESH


def block(sizes, field, cot, sw, tw, out, fg, sg, tg,
          xf, bf, ct, ac, gp, wf, wt, wb, tb, rb, rv, rs, fin,
          chan_s, chan_r, halo_s, halo_r, time_s, time_r, red_s, red_r):
    nh, ns, nc, scale = sizes
    frames, rows, own, cells = field.shape
    full = own * nc
    pad = tw.shape[0] // 2
    ntap = tw.shape[0]
    n = nh * ns
    chunk = rv.shape[1]
    s, b, c = lax.axis_index("shard"), lax.axis_index("sub"), lax.axis_index("chan")
    me = s * ns + b
    has_up, has_down = b > 0, b < ns - 1
    has_prev, has_next = s > 0, s < nh - 1
    up, down = lax.rem(b + ns - 1, ns), lax.rem(b + 1, ns)
    prev, nxt = lax.rem(s + nh - 1, nh), lax.rem(s + 1, nh)

    def peer(d):
        other = lax.rem(me + d, n)
        return other, {"shard": other // ns, "sub": lax.rem(other, ns)}

    barrier = pltpu.get_barrier_semaphore()

    def hello(device):
        pl.semaphore_signal(barrier, inc=1, device_id=device, device_id_type=MESH)

    for p in range(1, nc):
        chan = lax.rem(c + p, nc)
        hello({"chan": chan})

        @pl.when(has_up)
        def _():
            hello({"sub": up, "chan": chan})

        @pl.when(has_down)
        def _():
            hello({"sub": down, "chan": chan})

    def hello_peer(d, carry):
        hello(peer(d)[1])
        return carry

    lax.fori_loop(1, n, hello_peer, 0)

    def place(f, carry):
        for r in range(rows):
            xf[c, f, r + 1] = field[f, r]
            ct[f + pad, r] = cot[f, r]
        return carry

    lax.fori_loop(0, frames, place, 0)

    @pl.when(jnp.logical_not(has_up))
    def _():
        for q in range(nc):
            for f in range(frames):
                xf[q, f, 0] = jnp.zeros((own, cells), BF16)
                bf[q, f, 0] = jnp.zeros((own, cells), BF16)

    @pl.when(jnp.logical_not(has_down))
    def _():
        for q in range(nc):
            for f in range(frames):
                xf[q, f, rows + 1] = jnp.zeros((own, cells), BF16)
                bf[q, f, rows + 1] = jnp.zeros((own, cells), BF16)

    @pl.when(jnp.logical_not(has_prev))
    def _():
        for f in range(pad):
            for r in range(rows):
                ct[f, r] = jnp.zeros((own, cells), BF16)
                ac[f, r] = jnp.zeros((own, cells), BF16)

    @pl.when(jnp.logical_not(has_next))
    def _():
        for f in range(pad):
            for r in range(rows):
                ct[frames + pad + f, r] = jnp.zeros((own, cells), BF16)
                ac[frames + pad + f, r] = jnp.zeros((own, cells), BF16)

    mine = pl.ds(pl.multiple_of(c * own, own), own)
    taps_t = jnp.transpose(tw[...].astype(F32))
    for k in range(ntap):
        tb[k] = jnp.broadcast_to(taps_t[:, k : k + 1], (own, cells))
    for i in range(3):
        for j in range(3):
            wf[i, j * own : (j + 1) * own] = sw[i, j, mine]
            wt[...] = jnp.transpose(sw[i, j].astype(F32)).astype(BF16)
            wb[i, j * own : (j + 1) * own] = wt[mine]

    pl.semaphore_wait(
        barrier,
        n - 1 + (nc - 1) * (1 + has_up.astype(jnp.int32) + has_down.astype(jnp.int32)),
    )

    def remote(src, dst, ss, rr, device):
        return pltpu.make_async_remote_copy(
            src_ref=src, dst_ref=dst, send_sem=ss, recv_sem=rr,
            device_id=device, device_id_type=MESH,
        )

    def chan_copies(t, src, dst):
        return [
            remote(src, dst, chan_s.at[t, p - 1], chan_r.at[t, p - 1], {"chan": lax.rem(c + p, nc)})
            for p in range(1, nc)
        ]

    def up_copies(t, src, dst):
        return [
            remote(src, dst, halo_s.at[t, 0, p], halo_r.at[t, 0, p],
                   {"sub": up, "chan": lax.rem(c + p, nc)})
            for p in range(nc)
        ]

    def down_copies(t, src, dst):
        return [
            remote(src, dst, halo_s.at[t, 1, p], halo_r.at[t, 1, p],
                   {"sub": down, "chan": lax.rem(c + p, nc)})
            for p in range(nc)
        ]

    def run(cond, copies, what):
        @pl.when(cond)
        def _():
            for copy in copies:
                getattr(copy, what)()

    x_chan = chan_copies(0, field, xf.at[c, :, 1 : rows + 1])
    x_up = up_copies(0, field.at[:, 0], xf.at[c, :, rows + 1])
    x_down = down_copies(0, field.at[:, rows - 1], xf.at[c, :, 0])
    for copy in x_chan:
        copy.start()
    run(has_up, x_up, "start")
    run(has_down, x_down, "start")

    def time_copies(t, head, tail, buf):
        to_prev = remote(head, buf.at[frames + pad :], time_s.at[t, 0], time_r.at[t, 0], {"shard": prev})
        to_next = remote(tail, buf.at[:pad], time_s.at[t, 1], time_r.at[t, 1], {"shard": nxt})
        return [to_prev], [to_next]

    c_prev, c_next = time_copies(0, cot.at[:pad], cot.at[frames - pad :], ct)
    run(has_prev, c_prev, "start")
    run(has_next, c_next, "start")

    lane = lax.broadcasted_iota(jnp.int32, (own, cells), 1)

    def from_left(v):
        return jnp.where(lane == 0, 0.0, pltpu.roll(v, 1, 1))

    def from_right(v):
        return jnp.where(lane == cells - 1, 0.0, pltpu.roll(v, cells - 1, 1))

    def row_of(buf, f, r):
        return jnp.concatenate([buf[q, f, r] for q in range(nc)], axis=0)

    def rows_of(buf, f):
        return [row_of(buf, f, r) for r in range(rows + 2)]

    rb[...] = jnp.zeros(rb.shape, F32)

    for copy in x_chan:
        copy.wait_recv()
    run(has_down, x_up, "wait_recv")
    run(has_up, x_down, "wait_recv")

    def forward(f, carry):
        line = rows_of(xf, f)
        total = None
        for i in range(3):
            part = jnp.dot(wf[i], jnp.concatenate(line[i : i + rows], axis=1),
                           preferred_element_type=F32)
            total = part if total is None else total + part
        for r in range(rows):
            seg = total[:, r * cells : (r + 1) * cells]
            h = from_left(seg[:own]) + seg[own : 2 * own] + from_right(seg[2 * own :])
            hh = h * h
            t = jnp.tanh(ROOT * (h + CUBE * (hh * h)))
            half = 0.5 * (1.0 + t)
            ac[f + pad, r] = (h * half).astype(BF16)
            gp[f, r] = half + (0.5 * h) * (1.0 - t * t) * (ROOT * (1.0 + (3.0 * CUBE) * hh))
        return carry

    lax.fori_loop(0, frames, forward, 0)

    a_prev, a_next = time_copies(1, ac.at[pad : 2 * pad], ac.at[frames : frames + pad], ac)
    run(has_prev, a_prev, "start")
    run(has_next, a_next, "start")

    run(has_next, c_prev, "wait_recv")
    run(has_prev, c_next, "wait_recv")

    step = 16 if own % 16 == 0 else own
    ones = jnp.ones((8, cells), F32)

    def back(q):
        part = pl.ds(q * step, step)

        def body(r, sums):
            grads = [ct[g, r, part].astype(F32) for g in range(frames + 2 * pad)]
            sums = list(sums)
            for f in range(frames):
                act = ac[f + pad, r, part].astype(F32)
                total = None
                for k in range(ntap):
                    g = grads[f + 2 * pad - k]
                    term = tb[k, part] * g
                    total = term if total is None else total + term
                    sums[k] = sums[k] + act * g
                bt = total.astype(BF16).astype(F32)
                bf[c, f, r + 1, part] = (bt * gp[f, r, part]).astype(BF16)
            return tuple(sums)

        zero = jnp.zeros((step, cells), F32)
        return lax.fori_loop(0, rows, body, (zero,) * ntap)

    pieces = [back(q) for q in range(own // step)]

    g_chan = chan_copies(1, bf.at[c, :, 1 : rows + 1], bf.at[c, :, 1 : rows + 1])
    g_up = up_copies(1, bf.at[c, :, 1], bf.at[c, :, rows + 1])
    g_down = down_copies(1, bf.at[c, :, rows], bf.at[c, :, 0])
    for copy in g_chan:
        copy.start()
    run(has_up, g_up, "start")
    run(has_down, g_down, "start")

    base = 9 * own
    for k in range(ntap):
        whole = jnp.concatenate([piece[k] for piece in pieces], axis=0)
        line = lax.dot_general(ones, whole, (((1,), (1,)), ((), ())),
                               precision=lax.Precision.HIGHEST, preferred_element_type=F32)
        rb[base + k : base + k + 1, :own] = line[:1]

    def weight(f, carry):
        shifted = [[], [], []]
        for r in range(rows):
            v = bf[c, f, r + 1].astype(F32)
            shifted[0].append(from_right(v).astype(BF16))
            shifted[1].append(v.astype(BF16))
            shifted[2].append(from_left(v).astype(BF16))
        left = jnp.concatenate([jnp.concatenate(x, axis=1) for x in shifted], axis=0)
        line = rows_of(xf, f)
        for i in range(3):
            right = jnp.concatenate(line[i : i + rows], axis=1)
            rb[i * 3 * own : (i + 1) * 3 * own] += lax.dot_general(
                left, right, (((1,), (1,)), ((), ())), preferred_element_type=F32
            )
        return carry

    lax.fori_loop(0, frames, weight, 0)

    def scatter(d):
        other, device = peer(d)
        src = rb.at[pl.ds(pl.multiple_of(other * chunk, 8), chunk)]
        return remote(src, rv.at[d - 1], red_s.at[0, d - 1], red_r.at[0, d - 1], device)

    def gather(d):
        _, device = peer(d)
        dst = fin.at[pl.ds(pl.multiple_of(me * chunk, 8), chunk)]
        return remote(rs, dst, red_s.at[1, d - 1], red_r.at[1, d - 1], device)

    def each(make, what):
        def body(d, carry):
            getattr(make(d), what)()
            return carry

        lax.fori_loop(1, n, body, 0)

    each(scatter, "start")

    for copy in g_chan:
        copy.wait_recv()
    run(has_down, g_up, "wait_recv")
    run(has_up, g_down, "wait_recv")

    def backward(f, carry):
        line = rows_of(bf, f)
        total = None
        for i in range(3):
            part = jnp.dot(wb[i], jnp.concatenate(line[2 - i : 2 - i + rows], axis=1),
                           preferred_element_type=F32)
            total = part if total is None else total + part
        for r in range(rows):
            seg = total[:, r * cells : (r + 1) * cells]
            h = from_right(seg[:own]) + seg[own : 2 * own] + from_left(seg[2 * own :])
            fg[f, r] = (cot[f, r].astype(F32) + h).astype(BF16)
        return carry

    lax.fori_loop(0, frames, backward, 0)

    each(scatter, "wait_recv")

    here = pl.ds(pl.multiple_of(me * chunk, 8), chunk)
    total = lax.fori_loop(0, n - 1, lambda d, acc: acc + rv[d], rb[here]) * scale
    rs[...] = total
    fin[here] = total
    each(gather, "start")

    run(has_next, a_prev, "wait_recv")
    run(has_prev, a_next, "wait_recv")

    for q in range(own // step):
        part = pl.ds(q * step, step)

        def mix(r, carry, part=part):
            acts = [ac[g, r, part].astype(F32) for g in range(frames + 2 * pad)]
            for f in range(frames):
                total = None
                for k in range(ntap):
                    term = tb[k, part] * acts[f + k]
                    total = term if total is None else total + term
                mixed = total.astype(BF16).astype(F32)
                out[f, r, part] = (field[f, r, part].astype(F32) + mixed).astype(BF16)
            return carry

        lax.fori_loop(0, rows, mix, 0)

    each(gather, "wait_recv")
    for i in range(3):
        for j in range(3):
            at = (i * 3 + j) * own
            sg[i, j] = fin[at : at + own]
    tg[...] = fin[base : base + ntap, :own]

    for copy in x_chan + g_chan:
        copy.wait_send()
    run(has_up, x_up + g_up, "wait_send")
    run(has_down, x_down + g_down, "wait_send")
    run(has_prev, c_prev + a_prev, "wait_send")
    run(has_next, c_next + a_next, "wait_send")
    each(scatter, "wait_send")
    each(gather, "wait_send")


def on_device(field, cotangent, space_weight, time_weight):
    frames, rows, own, cells = field.shape
    nh, ns, nc = (lax.axis_size(a) for a in ("shard", "sub", "chan"))
    ntap = time_weight.shape[0]
    pad = ntap // 2
    full = own * nc
    n = nh * ns
    need = 9 * own + ntap
    chunk = -(-need // (8 * n)) * 8
    scale = float(frames * nh * rows * ns * cells) ** (-0.5)
    vmem = pl.BlockSpec(memory_space=pltpu.VMEM)
    dma = pltpu.SemaphoreType.DMA
    return pl.pallas_call(
        functools.partial(block, (nh, ns, nc, scale)),
        out_shape=(
            jax.ShapeDtypeStruct(field.shape, BF16),
            jax.ShapeDtypeStruct(field.shape, BF16),
            jax.ShapeDtypeStruct((3, 3, own, full), F32),
            jax.ShapeDtypeStruct((ntap, own), F32),
        ),
        in_specs=[vmem] * 4,
        out_specs=(vmem,) * 4,
        scratch_shapes=[
            pltpu.VMEM((nc, frames, rows + 2, own, cells), BF16),
            pltpu.VMEM((nc, frames, rows + 2, own, cells), BF16),
            pltpu.VMEM((frames + 2 * pad, rows, own, cells), BF16),
            pltpu.VMEM((frames + 2 * pad, rows, own, cells), BF16),
            pltpu.VMEM((frames, rows, own, cells), F32),
            pltpu.VMEM((3, 3 * own, full), BF16),
            pltpu.VMEM((full, full), BF16),
            pltpu.VMEM((3, 3 * own, full), BF16),
            pltpu.VMEM((ntap, own, cells), F32),
            pltpu.VMEM((n * chunk, full), F32),
            pltpu.VMEM((n - 1, chunk, full), F32),
            pltpu.VMEM((chunk, full), F32),
            pltpu.VMEM((n * chunk, full), F32),
            dma((2, nc - 1)),
            dma((2, nc - 1)),
            dma((2, 2, nc)),
            dma((2, 2, nc)),
            dma((2, 2)),
            dma((2, 2)),
            dma((2, n - 1)),
            dma((2, n - 1)),
        ],
        compiler_params=pltpu.CompilerParams(
            collective_id=0, has_side_effects=True, vmem_limit_bytes=60 * 1024 * 1024
        ),
    )(field, cotangent, space_weight, time_weight)


def solution(mesh):
    placed = (
        P(("groups", "shard"), "sub", "chan", None),
        P(("groups", "shard"), "sub", "chan", None),
        P(),
        P(None, "chan"),
    )
    return jax.shard_map(
        on_device,
        mesh=mesh,
        in_specs=placed,
        out_specs=(
            P(("groups", "shard"), "sub", "chan", None),
            P(("groups", "shard"), "sub", "chan", None),
            P("groups", None, "chan", None),
            P("groups", "chan"),
        ),
        check_vma=False,
    )
```

time: 163 us -> 34.4 us (0.21)
  waiting for transfers between devices: 76.4 us -> 0 us
  Pallas kernels: 0 us -> 29.6 us
  starting transfers between devices: 27.3 us -> 0 us
  blocking collectives: 25.9 us -> 0 us
  between operations: 14.4 us -> 0.65 us
  matrix products: 9.13 us -> 0 us
  other arithmetic: 5.67 us -> 0 us
    psum x1 -> x0, waiting for transfers between devices: 63.5 us -> none  [on_device(): lax.psum((space_part, time_part), ('shard', 'sub'))]
    pallas_call x0 -> x1, Pallas kernels: none -> 29.6 us  [on_device(): pl.pallas_call(functools.partial(block, (nh, ns, nc, scale)), out_shape=(...]
    psum x1 -> x0, blocking collectives: 21.3 us -> none  [on_device(): lax.psum((space_part, time_part), ('shard', 'sub'))]
    all_to_all x4 -> x0, starting transfers between devices: 15.3 us -> none  [the longest x2 8.24 us: to_time(): lax.all_to_all(values, 'shard', split_axis=1, concat_axis=0, tiled=True)]
    ppermute x4 -> x0, starting transfers between devices: 12 us -> none  [the longest x2 9.39 us: with_halo(): lax.ppermute(tail, axis, [(i, (i + 1) % count) for i in range(ends)])]
    dot_general x27 -> x0, matrix products: 9.13 us -> none  [the longest x9 3.67 us: on_device(): jnp.einsum('oc,frow->frcw', tap_cols[i, j], wide_grad[:, 2 - i:2 - i + ro...]
    all_to_all x4 -> x0, waiting for transfers between devices: 8.92 us -> none  [the longest x2 5.68 us: to_space(): lax.all_to_all(values, 'shard', split_axis=0, concat_axis=1, tiled=True)]
    all_gather x2 -> x0, blocking collectives: 4.59 us -> none  [widen(): gathered = lax.all_gather(rimmed, 'chan', axis=2, tiled=True)]
  transfers between devices with their start and end apart: 9 -> 0, of which waited for: 4 -> 0; matrix products, arithmetic and copies ran while one was open for 7% -> 0% of each run, Pallas kernels for 0% -> 0%
where the time goes in v1:
time: 34.4 us; the launch traced here: 34.2 us
  Pallas kernels  29.6 us (86%)
  local copies, waits for them, and re-layouts  3.96 us (12%)
  between operations  0.65 us (2%)
    pallas_call x1, Pallas kernels, on_device(): pl.pallas_call(functools.partial(block, (nh, ns, nc, scale)), out_shape=(...  29.6 us
    unnamed x10, local copies, waits for them, and re-layouts  3.96 us

profile of v1, /device:TPU:0, one launch (start us, length us, event | category | flops | bytes accessed | tf_op | source)
XLA Modules:
  0.0 34.2 jit_solution(1435562546880908580)
XLA Ops:
  0.6 29.6 %shard_map.75 = (bf16[4,4,48,128]{3,2,1,0:T(8,128)(2,1)}, bf16[4,4,48,128]{3,2,1,0:T(8,128)(2,1)}, f32[3,3,48,96]{3,2,1,0:T(8,128)}, f32[9,48]{1,0:T(8,128)}) custom-call(bf16[4,4,48,128]{3,2,1,0:T(8,128)(2,1)} %field.1, bf16[4,4,48,128]{3,2,1,0:T(8,128)(2,1)} %cot.1, bf16[3,3,96,96]{3,2,1,0:T(8,128)(2,1)} %sw.1, bf16[9,48]{1,0:T(8,128)(2,1)} %tw.1), custom_call_target="tpu_custom_call" | custom-call | tf_op jit(solution)/shard_map/pallas_call | solution.py:363
  30.2 0.0 copy-start.1
  30.2 1.7 %copy.12 = bf16[4,4,48,128]{3,2,1,0:T(8,128)(2,1)} copy(bf16[4,4,48,128]{3,2,1,0:T(8,128)(2,1)} %get-tuple-element.8) | data formatting | bytes 393216
  31.9 0.0 copy-done.1
  31.9 0.0 copy-start
  31.9 0.7 %copy.13 = bf16[4,4,48,128]{3,2,1,0:T(8,128)(2,1)} copy(bf16[4,4,48,128]{3,2,1,0:T(8,128)(2,1)S(1)} %copy-done.1) | data formatting | bytes 393216
  32.6 0.3 copy-done
  32.9 0.0 copy-start.2
  32.9 0.7 %copy.14 = f32[3,3,48,96]{3,2,1,0:T(8,128)} copy(f32[3,3,48,96]{3,2,1,0:T(8,128)S(1)} %copy-done) | data formatting | bytes 331776
  33.6 0.0 copy-done.2
  33.6 0.6 %copy.15 = f32[9,48]{1,0:T(8,128)} copy(f32[9,48]{1,0:T(8,128)S(1)} %copy-done.2) | data formatting | bytes 3456
Async XLA Ops:
  30.2 1.7 %copy-start.1 = (bf16[4,4,48,128]{3,2,1,0:T(8,128)(2,1)S(1)}, bf16[4,4,48,128]{3,2,1,0:T(8,128)(2,1)}, u32[]{:S(2)}) copy-start(bf16[4,4,48,128]{3,2,1,0:T(8,128)(2,1)} %get-tuple-element.9) | copy-start | bytes 589828
  31.9 1.0 %copy-start = (f32[3,3,48,96]{3,2,1,0:T(8,128)S(1)}, f32[3,3,48,96]{3,2,1,0:T(8,128)}, u32[]{:S(2)}) copy-start(f32[3,3,48,96]{3,2,1,0:T(8,128)} %get-tuple-element.10) | copy-start | bytes 497668
  32.9 0.7 %copy-start.2 = (f32[9,48]{1,0:T(8,128)S(1)}, f32[9,48]{1,0:T(8,128)}, u32[]{:S(2)}) copy-start(f32[9,48]{1,0:T(8,128)} %get-tuple-element.11) | copy-start | bytes 5188

commit v2 on v1

--- a/solution.py
+++ b/solution.py
@@ -17,7 +17,7 @@
 
 def block(sizes, field, cot, sw, tw, out, fg, sg, tg,
           xf, bf, ct, ac, gp, wf, wt, wb, tb, rb, rv, rs, fin,
-          chan_s, chan_r, halo_s, halo_r, time_s, time_r, red_s, red_r):
+          swv, twv, load_s, chan_s, chan_r, halo_s, halo_r, time_s, time_r, red_s, red_r):
     nh, ns, nc, scale = sizes
     frames, rows, own, cells = field.shape
     full = own * nc
@@ -59,13 +59,17 @@
 
     lax.fori_loop(1, n, hello_peer, 0)
 
-    def place(f, carry):
-        for r in range(rows):
-            xf[c, f, r + 1] = field[f, r]
-            ct[f + pad, r] = cot[f, r]
-        return carry
-
-    lax.fori_loop(0, frames, place, 0)
+    loads = [
+        pltpu.make_async_copy(src, dst, load_s.at[at])
+        for at, (src, dst) in enumerate((
+            (tw, twv),
+            (sw, swv),
+            (field, xf.at[c, :, 1 : rows + 1]),
+            (cot, ct.at[pad : pad + frames]),
+        ))
+    ]
+    for load in loads:
+        load.start()
 
     @pl.when(jnp.logical_not(has_up))
     def _():
@@ -96,19 +100,12 @@
                 ac[frames + pad + f, r] = jnp.zeros((own, cells), BF16)
 
     mine = pl.ds(pl.multiple_of(c * own, own), own)
-    taps_t = jnp.transpose(tw[...].astype(F32))
-    for k in range(ntap):
-        tb[k] = jnp.broadcast_to(taps_t[:, k : k + 1], (own, cells))
-    for i in range(3):
-        for j in range(3):
-            wf[i, j * own : (j + 1) * own] = sw[i, j, mine]
-            wt[...] = jnp.transpose(sw[i, j].astype(F32)).astype(BF16)
-            wb[i, j * own : (j + 1) * own] = wt[mine]
-
-    pl.semaphore_wait(
-        barrier,
-        n - 1 + (nc - 1) * (1 + has_up.astype(jnp.int32) + has_down.astype(jnp.int32)),
-    )
+
+    with jax.named_scope("hello"):
+        pl.semaphore_wait(
+            barrier,
+            n - 1 + (nc - 1) * (1 + has_up.astype(jnp.int32) + has_down.astype(jnp.int32)),
+        )
 
     def remote(src, dst, ss, rr, device):
         return pltpu.make_async_remote_copy(
@@ -159,6 +156,23 @@
     run(has_prev, c_prev, "start")
     run(has_next, c_next, "start")
 
+    with jax.named_scope("prep"):
+        for load in loads[:2]:
+            load.wait()
+        taps_t = jnp.transpose(twv[...].astype(F32))
+        for k in range(ntap):
+            tb[k] = jnp.broadcast_to(taps_t[:, k : k + 1], (own, cells))
+        for i in range(3):
+            for j in range(3):
+                wf[i, j * own : (j + 1) * own] = swv[i, j, mine]
+                wt[i, j] = jnp.transpose(swv[i, j].astype(F32)).astype(BF16)
+        for i in range(3):
+            for j in range(3):
+                wb[i, j * own : (j + 1) * own] = wt[i, j, mine]
+        rb[...] = jnp.zeros(rb.shape, F32)
+        for load in loads[2:]:
+            load.wait()
+
     lane = lax.broadcasted_iota(jnp.int32, (own, cells), 1)
 
     def from_left(v):
@@ -173,12 +187,11 @@
     def rows_of(buf, f):
         return [row_of(buf, f, r) for r in range(rows + 2)]
 
-    rb[...] = jnp.zeros(rb.shape, F32)
-
-    for copy in x_chan:
-        copy.wait_recv()
-    run(has_down, x_up, "wait_recv")
-    run(has_up, x_down, "wait_recv")
+    with jax.named_scope("wait_x"):
+        for copy in x_chan:
+            copy.wait_recv()
+        run(has_down, x_up, "wait_recv")
+        run(has_up, x_down, "wait_recv")
 
     def forward(f, carry):
         line = rows_of(xf, f)
@@ -197,14 +210,16 @@
             gp[f, r] = half + (0.5 * h) * (1.0 - t * t) * (ROOT * (1.0 + (3.0 * CUBE) * hh))
         return carry
 
-    lax.fori_loop(0, frames, forward, 0)
+    with jax.named_scope("fwd"):
+        lax.fori_loop(0, frames, forward, 0)
 
     a_prev, a_next = time_copies(1, ac.at[pad : 2 * pad], ac.at[frames : frames + pad], ac)
     run(has_prev, a_prev, "start")
     run(has_next, a_next, "start")
 
-    run(has_next, c_prev, "wait_recv")
-    run(has_prev, c_next, "wait_recv")
+    with jax.named_scope("wait_c"):
+        run(has_next, c_prev, "wait_recv")
+        run(has_prev, c_next, "wait_recv")
 
     step = 16 if own % 16 == 0 else own
     ones = jnp.ones((8, cells), F32)
@@ -230,7 +245,8 @@
         zero = jnp.zeros((step, cells), F32)
         return lax.fori_loop(0, rows, body, (zero,) * ntap)
 
-    pieces = [back(q) for q in range(own // step)]
+    with jax.named_scope("back"):
+        pieces = [back(q) for q in range(own // step)]
 
     g_chan = chan_copies(1, bf.at[c, :, 1 : rows + 1], bf.at[c, :, 1 : rows + 1])
     g_up = up_copies(1, bf.at[c, :, 1], bf.at[c, :, rows + 1])
@@ -263,7 +279,8 @@
             )
         return carry
 
-    lax.fori_loop(0, frames, weight, 0)
+    with jax.named_scope("wgt"):
+        lax.fori_loop(0, frames, weight, 0)
 
     def scatter(d):
         other, device = peer(d)
@@ -284,10 +301,11 @@
 
     each(scatter, "start")
 
-    for copy in g_chan:
-        copy.wait_recv()
-    run(has_down, g_up, "wait_recv")
-    run(has_up, g_down, "wait_recv")
+    with jax.named_scope("wait_g"):
+        for copy in g_chan:
+            copy.wait_recv()
+        run(has_down, g_up, "wait_recv")
+        run(has_up, g_down, "wait_recv")
 
     def backward(f, carry):
         line = rows_of(bf, f)
@@ -299,12 +317,14 @@
         for r in range(rows):
             seg = total[:, r * cells : (r + 1) * cells]
             h = from_right(seg[:own]) + seg[own : 2 * own] + from_left(seg[2 * own :])
-            fg[f, r] = (cot[f, r].astype(F32) + h).astype(BF16)
+            fg[f, r] = (ct[f + pad, r].astype(F32) + h).astype(BF16)
         return carry
 
-    lax.fori_loop(0, frames, backward, 0)
-
-    each(scatter, "wait_recv")
+    with jax.named_scope("bwd"):
+        lax.fori_loop(0, frames, backward, 0)
+
+    with jax.named_scope("wait_rs"):
+        each(scatter, "wait_recv")
 
     here = pl.ds(pl.multiple_of(me * chunk, 8), chunk)
     total = lax.fori_loop(0, n - 1, lambda d, acc: acc + rv[d], rb[here]) * scale
@@ -312,8 +332,9 @@
     fin[here] = total
     each(gather, "start")
 
-    run(has_next, a_prev, "wait_recv")
-    run(has_prev, a_next, "wait_recv")
+    with jax.named_scope("wait_a"):
+        run(has_next, a_prev, "wait_recv")
+        run(has_prev, a_next, "wait_recv")
 
     for q in range(own // step):
         part = pl.ds(q * step, step)
@@ -326,12 +347,13 @@
                     term = tb[k, part] * acts[f + k]
                     total = term if total is None else total + term
                 mixed = total.astype(BF16).astype(F32)
-                out[f, r, part] = (field[f, r, part].astype(F32) + mixed).astype(BF16)
+                out[f, r, part] = (xf[c, f, r + 1, part].astype(F32) + mixed).astype(BF16)
             return carry
 
         lax.fori_loop(0, rows, mix, 0)
 
-    each(gather, "wait_recv")
+    with jax.named_scope("wait_ag"):
+        each(gather, "wait_recv")
     for i in range(3):
         for j in range(3):
             at = (i * 3 + j) * own
@@ -346,6 +368,15 @@
     run(has_next, c_next + a_next, "wait_send")
     each(scatter, "wait_send")
     each(gather, "wait_send")
+
+
+def ship(*refs):
+    sems = refs[8]
+    copies = [pltpu.make_async_copy(refs[i], refs[i + 4], sems.at[i]) for i in range(4)]
+    for copy in copies:
+        copy.start()
+    for copy in copies:
+        copy.wait()
 
 
 def on_device(field, cotangent, space_weight, time_weight):
@@ -360,15 +391,18 @@
     scale = float(frames * nh * rows * ns * cells) ** (-0.5)
     vmem = pl.BlockSpec(memory_space=pltpu.VMEM)
     dma = pltpu.SemaphoreType.DMA
-    return pl.pallas_call(
+    limit = 20 * 2**20 if rows * frames <= 16 else 56 * 2**20
+    hbm = pl.BlockSpec(memory_space=pltpu.HBM)
+    shapes = (
+        (field.shape, BF16),
+        (field.shape, BF16),
+        ((3, 3, own, full), F32),
+        ((ntap, own), F32),
+    )
+    held = pl.pallas_call(
         functools.partial(block, (nh, ns, nc, scale)),
-        out_shape=(
-            jax.ShapeDtypeStruct(field.shape, BF16),
-            jax.ShapeDtypeStruct(field.shape, BF16),
-            jax.ShapeDtypeStruct((3, 3, own, full), F32),
-            jax.ShapeDtypeStruct((ntap, own), F32),
-        ),
-        in_specs=[vmem] * 4,
+        out_shape=tuple(pltpu.VMEM(*x) for x in shapes),
+        in_specs=[hbm] * 4,
         out_specs=(vmem,) * 4,
         scratch_shapes=[
             pltpu.VMEM((nc, frames, rows + 2, own, cells), BF16),
@@ -377,13 +411,16 @@
             pltpu.VMEM((frames + 2 * pad, rows, own, cells), BF16),
             pltpu.VMEM((frames, rows, own, cells), F32),
             pltpu.VMEM((3, 3 * own, full), BF16),
-            pltpu.VMEM((full, full), BF16),
+            pltpu.VMEM((3, 3, full, full), BF16),
             pltpu.VMEM((3, 3 * own, full), BF16),
             pltpu.VMEM((ntap, own, cells), F32),
             pltpu.VMEM((n * chunk, full), F32),
             pltpu.VMEM((n - 1, chunk, full), F32),
             pltpu.VMEM((chunk, full), F32),
             pltpu.VMEM((n * chunk, full), F32),
+            pltpu.VMEM(space_weight.shape, BF16),
+            pltpu.VMEM(time_weight.shape, BF16),
+            dma((4,)),
             dma((2, nc - 1)),
             dma((2, nc - 1)),
             dma((2, 2, nc)),
@@ -394,9 +431,16 @@
             dma((2, n - 1)),
         ],
         compiler_params=pltpu.CompilerParams(
-            collective_id=0, has_side_effects=True, vmem_limit_bytes=60 * 1024 * 1024
+            collective_id=0, has_side_effects=True, vmem_limit_bytes=limit
         ),
-    )(field, cotangent, space_weight, time_weight)
+    )(*(pltpu.with_memory_space_constraint(x, pltpu.HBM) for x in (field, cotangent, space_weight, time_weight)))
+    return pl.pallas_call(
+        ship,
+        out_shape=tuple(jax.ShapeDtypeStruct(*x) for x in shapes),
+        in_specs=[vmem] * 4,
+        out_specs=(hbm,) * 4,
+        scratch_shapes=[dma((4,))],
+    )(*(pltpu.with_memory_space_constraint(x, pltpu.VMEM) for x in held))
 
 
 def solution(mesh):

time: 34.4 us -> 29.6 us (0.86)
  local copies, waits for them, and re-layouts: 3.96 us -> 0 us
  Pallas kernels: 29.6 us -> 28.8 us
    unnamed x10 -> x0, local copies, waits for them, and re-layouts: 3.96 us -> none
    pallas_call x1 -> x2, Pallas kernels: 29.6 us -> 28.8 us  [the longest x1 28 us: on_device(): pl.pallas_call(functools.partial(block, (nh, ns, nc, scale)), out_shape=t...]
where the time goes in v2:
time: 29.6 us; the launch traced here: 29.5 us
  Pallas kernels  28.8 us (97%)
  between operations  0.64 us (2%)
    pallas_call x1, Pallas kernels, on_device(): pl.pallas_call(functools.partial(block, (nh, ns, nc, scale)), out_shape=t...  28 us
    pallas_call x1, Pallas kernels, on_device(): pl.pallas_call(ship, out_shape=tuple((jax.ShapeDtypeStruct(*x) for x in s...  0.85 us

profile of v2, /device:TPU:0, one launch (start us, length us, event | category | flops | bytes accessed | tf_op | source)
XLA Modules:
  0.0 29.5 jit_solution(8773052615747205590)
XLA Ops:
  0.6 28.0 %shard_map.75 = (bf16[4,4,48,128]{3,2,1,0:T(8,128)(2,1)S(1)}, bf16[4,4,48,128]{3,2,1,0:T(8,128)(2,1)S(1)}, f32[3,3,48,96]{3,2,1,0:T(8,128)S(1)}, f32[9,48]{1,0:T(8,128)S(1)}) custom-call(bf16[4,4,48,128]{3,2,1,0:T(8,128)(2,1)} %field.1, bf16[4,4,48,128]{3,2,1,0:T(8,128)(2,1)} %cot.1, bf16[3,3,96,96]{3,2,1,0:T(8,128)(2,1)} %sw.1, bf16[9,48]{1,0:T(8,128)(2,1)} %tw.1), custom_call_target="tpu_custom_call" | custom-call | tf_op jit(solution)/shard_map/pallas_call | solution.py:402
  28.6 0.9 %shard_map.76 = (bf16[4,4,48,128]{3,2,1,0:T(8,128)(2,1)}, bf16[4,4,48,128]{3,2,1,0:T(8,128)(2,1)}, f32[3,3,48,96]{3,2,1,0:T(8,128)}, f32[9,48]{1,0:T(8,128)}) custom-call(bf16[4,4,48,128]{3,2,1,0:T(8,128)(2,1)S(1)} %get-tuple-element.8.refs_0_, bf16[4,4,48,128]{3,2,1,0:T(8,128)(2,1)S(1)} %get-tuple-element.9.refs_1_, ...), custom_call_target="tpu_custom_call" | custom-call | tf_op jit(solution)/shard_map/pallas_call | solution.py:437

commit v3 on v2

--- a/solution.py
+++ b/solution.py
@@ -9,15 +9,14 @@
 
 F32 = jnp.float32
 BF16 = jnp.bfloat16
-WIRE = jnp.float32
 ROOT = 0.7978845608028654
 CUBE = 0.044715
 MESH = pl.DeviceIdType.MESH
 
 
-def block(sizes, field, cot, sw, tw, out, fg, sg, tg,
-          xf, bf, ct, ac, gp, wf, wt, wb, tb, rb, rv, rs, fin,
-          swv, twv, load_s, chan_s, chan_r, halo_s, halo_r, time_s, time_r, red_s, red_r):
+def block(sizes, plan, field, cot, sw, tw, out, fg, sg, tg,
+          xf, bf, ct, ac, gp, wf, wt, wb, tb, rb, rbb, rv, rs, fin,
+          swv, twv, ready, load_s, chan_s, chan_r, halo_s, halo_r, time_s, time_r, red_s, red_r):
     nh, ns, nc, scale = sizes
     frames, rows, own, cells = field.shape
     full = own * nc
@@ -41,23 +40,41 @@
     def hello(device):
         pl.semaphore_signal(barrier, inc=1, device_id=device, device_id_type=MESH)
 
+    def at(**where):
+        return where
+
+    edges = [
+        (has_up, at(sub=up)),
+        (has_down, at(sub=down)),
+        (has_prev, at(shard=prev)),
+        (has_next, at(shard=nxt)),
+    ]
+    sides = sum(has.astype(jnp.int32) for has, _ in edges)
+    across = has_up.astype(jnp.int32) + has_down.astype(jnp.int32)
+
     for p in range(1, nc):
-        chan = lax.rem(c + p, nc)
-        hello({"chan": chan})
-
-        @pl.when(has_up)
-        def _():
-            hello({"sub": up, "chan": chan})
-
-        @pl.when(has_down)
-        def _():
-            hello({"sub": down, "chan": chan})
-
-    def hello_peer(d, carry):
-        hello(peer(d)[1])
-        return carry
-
-    lax.fori_loop(1, n, hello_peer, 0)
+        hello(at(chan=lax.rem(c + p, nc)))
+    for has, where in edges:
+        @pl.when(has)
+        def _(where=where):
+            hello(where)
+            if "sub" in where:
+                for p in range(1, nc):
+                    hello(at(chan=lax.rem(c + p, nc), **where))
+
+    rounds = nh + ns - 3
+
+    def tell(t):
+        for has, where in edges:
+            @pl.when(has)
+            def _(where=where):
+                pl.semaphore_signal(ready.at[t], inc=1, device_id=where, device_id_type=MESH)
+
+    def heard(t):
+        if t < rounds:
+            pl.semaphore_wait(ready.at[t], sides)
+            if t + 1 < rounds:
+                tell(t + 1)
 
     loads = [
         pltpu.make_async_copy(src, dst, load_s.at[at])
@@ -104,8 +121,10 @@
     with jax.named_scope("hello"):
         pl.semaphore_wait(
             barrier,
-            n - 1 + (nc - 1) * (1 + has_up.astype(jnp.int32) + has_down.astype(jnp.int32)),
+            nc - 1 + sides + (nc - 1) * across,
         )
+    if rounds > 0:
+        tell(0)
 
     def remote(src, dst, ss, rr, device):
         return pltpu.make_async_remote_copy(
@@ -210,16 +229,25 @@
             gp[f, r] = half + (0.5 * h) * (1.0 - t * t) * (ROOT * (1.0 + (3.0 * CUBE) * hh))
         return carry
 
+    heard(0)
     with jax.named_scope("fwd"):
         lax.fori_loop(0, frames, forward, 0)
 
-    a_prev, a_next = time_copies(1, ac.at[pad : 2 * pad], ac.at[frames : frames + pad], ac)
-    run(has_prev, a_prev, "start")
-    run(has_next, a_next, "start")
-
+    heard(1)
     with jax.named_scope("wait_c"):
         run(has_next, c_prev, "wait_recv")
         run(has_prev, c_next, "wait_recv")
+
+    half = max(rows // 2, 1)
+    a_prev, a_next = [], []
+    for t, part in ((1, slice(0, half)), (2, slice(half, rows))):
+        to_prev, to_next = time_copies(
+            t, ac.at[pad : 2 * pad, part], ac.at[frames : frames + pad, part], ac.at[:, part]
+        )
+        a_prev += to_prev
+        a_next += to_next
+    run(has_prev, a_prev[:1], "start")
+    run(has_next, a_next[:1], "start")
 
     step = 16 if own % 16 == 0 else own
     ones = jnp.ones((8, cells), F32)
@@ -246,7 +274,7 @@
         return lax.fori_loop(0, rows, body, (zero,) * ntap)
 
     with jax.named_scope("back"):
-        pieces = [back(q) for q in range(own // step)]
+        sums = [back(q) for q in range(own // step)]
 
     g_chan = chan_copies(1, bf.at[c, :, 1 : rows + 1], bf.at[c, :, 1 : rows + 1])
     g_up = up_copies(1, bf.at[c, :, 1], bf.at[c, :, rows + 1])
@@ -258,7 +286,7 @@
 
     base = 9 * own
     for k in range(ntap):
-        whole = jnp.concatenate([piece[k] for piece in pieces], axis=0)
+        whole = jnp.concatenate([piece[k] for piece in sums], axis=0)
         line = lax.dot_general(ones, whole, (((1,), (1,)), ((), ())),
                                precision=lax.Precision.HIGHEST, preferred_element_type=F32)
         rb[base + k : base + k + 1, :own] = line[:1]
@@ -274,7 +302,7 @@
         line = rows_of(xf, f)
         for i in range(3):
             right = jnp.concatenate(line[i : i + rows], axis=1)
-            rb[i * 3 * own : (i + 1) * 3 * own] += lax.dot_general(
+            rb[i * 3 * own : (i + 1) * 3 * own, :full] += lax.dot_general(
                 left, right, (((1,), (1,)), ((), ())), preferred_element_type=F32
             )
         return carry
@@ -284,12 +312,12 @@
 
     def scatter(d):
         other, device = peer(d)
-        src = rb.at[pl.ds(pl.multiple_of(other * chunk, 8), chunk)]
+        src = rbb.at[pl.ds(pl.multiple_of(other * chunk, 16), chunk)]
         return remote(src, rv.at[d - 1], red_s.at[0, d - 1], red_r.at[0, d - 1], device)
 
     def gather(d):
         _, device = peer(d)
-        dst = fin.at[pl.ds(pl.multiple_of(me * chunk, 8), chunk)]
+        dst = fin.at[pl.ds(pl.multiple_of(me * chunk, 16), chunk)]
         return remote(rs, dst, red_s.at[1, d - 1], red_r.at[1, d - 1], device)
 
     def each(make, what):
@@ -299,7 +327,28 @@
 
         lax.fori_loop(1, n, body, 0)
 
+    spare, pieces, extra = plan
+    packed = rb.shape[0] - extra
+    if packed < rbb.shape[0]:
+        rbb[packed:] = jnp.zeros((rbb.shape[0] - packed, rbb.shape[1]), BF16)
+    if pieces:
+        lanes = rb.shape[1]
+        place = lax.broadcasted_iota(jnp.int32, (extra, lanes), 1)
+        tail = rb[packed:]
+        for t in range(pieces):
+            mixed = jnp.where(
+                place < full,
+                rb[t * extra : (t + 1) * extra],
+                pltpu.roll(tail, (full - t * spare) % lanes, 1),
+            )
+            rbb[t * extra : (t + 1) * extra] = mixed.astype(BF16)
+    else:
+        rbb[:packed] = rb[...].astype(BF16)
+    for t in range(2, rounds):
+        heard(t)
     each(scatter, "start")
+    run(has_prev, a_prev[1:], "start")
+    run(has_next, a_next[1:], "start")
 
     with jax.named_scope("wait_g"):
         for copy in g_chan:
@@ -326,10 +375,10 @@
     with jax.named_scope("wait_rs"):
         each(scatter, "wait_recv")
 
-    here = pl.ds(pl.multiple_of(me * chunk, 8), chunk)
-    total = lax.fori_loop(0, n - 1, lambda d, acc: acc + rv[d], rb[here]) * scale
-    rs[...] = total
-    fin[here] = total
+    here = pl.ds(pl.multiple_of(me * chunk, 16), chunk)
+    total = lax.fori_loop(0, n - 1, lambda d, acc: acc + rv[d].astype(F32), rbb[here].astype(F32)) * scale
+    rs[...] = total.astype(BF16)
+    fin[here] = total.astype(BF16)
     each(gather, "start")
 
     with jax.named_scope("wait_a"):
@@ -354,11 +403,21 @@
 
     with jax.named_scope("wait_ag"):
         each(gather, "wait_recv")
+    if pieces:
+        last = None
+        for t in reversed(range(pieces)):
+            v = fin[t * extra : (t + 1) * extra].astype(F32)
+            rb[t * extra : (t + 1) * extra] = v
+            v = pltpu.roll(v, (t * spare - full) % lanes, 1)
+            last = v if last is None else jnp.where(place < (t + 1) * spare, v, last)
+        rb[packed:] = last
+    else:
+        rb[...] = fin[:packed].astype(F32)
     for i in range(3):
         for j in range(3):
-            at = (i * 3 + j) * own
-            sg[i, j] = fin[at : at + own]
-    tg[...] = fin[base : base + ntap, :own]
+            top = (i * 3 + j) * own
+            sg[i, j] = rb[top : top + own, :full]
+    tg[...] = rb[base : base + ntap, :own]
 
     for copy in x_chan + g_chan:
         copy.wait_send()
@@ -387,7 +446,15 @@
     full = own * nc
     n = nh * ns
     need = 9 * own + ntap
-    chunk = -(-need // (8 * n)) * 8
+    lanes = -(-full // 128) * 128
+    spare = lanes - full
+    if spare and full % spare == 0:
+        pieces = full // spare
+        extra = -(-need // (16 * (pieces + 1))) * 16
+        packed = extra * pieces
+    else:
+        pieces, extra, packed = 0, 0, -(-need // 16) * 16
+    chunk = -(-packed // (16 * n)) * 16
     scale = float(frames * nh * rows * ns * cells) ** (-0.5)
     vmem = pl.BlockSpec(memory_space=pltpu.VMEM)
     dma = pltpu.SemaphoreType.DMA
@@ -400,7 +467,7 @@
         ((ntap, own), F32),
     )
     held = pl.pallas_call(
-        functools.partial(block, (nh, ns, nc, scale)),
+        functools.partial(block, (nh, ns, nc, scale), (spare, pieces, extra)),
         out_shape=tuple(pltpu.VMEM(*x) for x in shapes),
         in_specs=[hbm] * 4,
         out_specs=(vmem,) * 4,
@@ -414,19 +481,21 @@
             pltpu.VMEM((3, 3, full, full), BF16),
             pltpu.VMEM((3, 3 * own, full), BF16),
             pltpu.VMEM((ntap, own, cells), F32),
-            pltpu.VMEM((n * chunk, full), F32),
-            pltpu.VMEM((n - 1, chunk, full), F32),
-            pltpu.VMEM((chunk, full), F32),
-            pltpu.VMEM((n * chunk, full), F32),
+            pltpu.VMEM((packed + extra, lanes), F32),
+            pltpu.VMEM((n * chunk, lanes), BF16),
+            pltpu.VMEM((n - 1, chunk, lanes), BF16),
+            pltpu.VMEM((chunk, lanes), BF16),
+            pltpu.VMEM((n * chunk, lanes), BF16),
             pltpu.VMEM(space_weight.shape, BF16),
             pltpu.VMEM(time_weight.shape, BF16),
+            pltpu.SemaphoreType.REGULAR((max(nh + ns - 3, 1),)),
             dma((4,)),
             dma((2, nc - 1)),
             dma((2, nc - 1)),
             dma((2, 2, nc)),
             dma((2, 2, nc)),
-            dma((2, 2)),
-            dma((2, 2)),
+            dma((3, 2)),
+            dma((3, 2)),
             dma((2, n - 1)),
             dma((2, n - 1)),
         ],

time: 29.6 us -> 24.8 us (0.84)
  Pallas kernels: 28.8 us -> 24 us
    pallas_call x1, Pallas kernels: 28 us -> 23.1 us  [on_device(): pl.pallas_call(functools.partial(block, (nh, ns, nc, scale), (spare, piec...]
where the time goes in v3:
time: 24.8 us; the launch traced here: 24.6 us
  Pallas kernels  24 us (97%)
  between operations  0.64 us (3%)
    pallas_call x1, Pallas kernels, on_device(): pl.pallas_call(functools.partial(block, (nh, ns, nc, scale), (spare, piec...  23.1 us
    pallas_call x1, Pallas kernels, on_device(): pl.pallas_call(ship, out_shape=tuple((jax.ShapeDtypeStruct(*x) for x in s...  0.85 us

profile of v3, /device:TPU:0, one launch (start us, length us, event | category | flops | bytes accessed | tf_op | source)
XLA Modules:
  0.0 24.6 jit_solution(3289656936720744504)
XLA Ops:
  0.6 23.1 %shard_map.75 = (bf16[4,4,48,128]{3,2,1,0:T(8,128)(2,1)S(1)}, bf16[4,4,48,128]{3,2,1,0:T(8,128)(2,1)S(1)}, f32[3,3,48,96]{3,2,1,0:T(8,128)S(1)}, f32[9,48]{1,0:T(8,128)S(1)}) custom-call(bf16[4,4,48,128]{3,2,1,0:T(8,128)(2,1)} %field.1, bf16[4,4,48,128]{3,2,1,0:T(8,128)(2,1)} %cot.1, bf16[3,3,96,96]{3,2,1,0:T(8,128)(2,1)} %sw.1, bf16[9,48]{1,0:T(8,128)(2,1)} %tw.1), custom_call_target="tpu_custom_call" | custom-call | tf_op jit(solution)/shard_map/pallas_call | solution.py:469
  23.8 0.9 %shard_map.76 = (bf16[4,4,48,128]{3,2,1,0:T(8,128)(2,1)}, bf16[4,4,48,128]{3,2,1,0:T(8,128)(2,1)}, f32[3,3,48,96]{3,2,1,0:T(8,128)}, f32[9,48]{1,0:T(8,128)}) custom-call(bf16[4,4,48,128]{3,2,1,0:T(8,128)(2,1)S(1)} %get-tuple-element.8.refs_0_, bf16[4,4,48,128]{3,2,1,0:T(8,128)(2,1)S(1)} %get-tuple-element.9.refs_1_, ...), custom_call_target="tpu_custom_call" | custom-call | tf_op jit(solution)/shard_map/pallas_call | solution.py:506

commit v4 on v3

--- a/solution.py
+++ b/solution.py
@@ -24,6 +24,7 @@
     ntap = tw.shape[0]
     n = nh * ns
     chunk = rv.shape[1]
+    parts = row_parts(rows)
     s, b, c = lax.axis_index("shard"), lax.axis_index("sub"), lax.axis_index("chan")
     me = s * ns + b
     has_up, has_down = b > 0, b < ns - 1
@@ -171,9 +172,15 @@
         to_next = remote(tail, buf.at[:pad], time_s.at[t, 1], time_r.at[t, 1], {"shard": nxt})
         return [to_prev], [to_next]
 
-    c_prev, c_next = time_copies(0, cot.at[:pad], cot.at[frames - pad :], ct)
-    run(has_prev, c_prev, "start")
-    run(has_next, c_next, "start")
+    c_prev, c_next = [], []
+    for t, (lo, hi) in enumerate(parts):
+        to_prev, to_next = time_copies(
+            t, cot.at[:pad, lo:hi], cot.at[frames - pad :, lo:hi], ct.at[:, lo:hi]
+        )
+        c_prev += to_prev
+        c_next += to_next
+        run(has_prev, to_prev, "start")
+        run(has_next, to_next, "start")
 
     with jax.named_scope("prep"):
         for load in loads[:2]:
@@ -231,28 +238,20 @@
 
     heard(0)
     with jax.named_scope("fwd"):
-        lax.fori_loop(0, frames, forward, 0)
+        lax.fori_loop(0, frames, forward, 0, unroll=True)
 
     heard(1)
-    with jax.named_scope("wait_c"):
-        run(has_next, c_prev, "wait_recv")
-        run(has_prev, c_next, "wait_recv")
-
     half = max(rows // 2, 1)
     a_prev, a_next = [], []
-    for t, part in ((1, slice(0, half)), (2, slice(half, rows))):
+    for t, part in ((len(parts), slice(0, half)), (len(parts) + 1, slice(half, rows))):
         to_prev, to_next = time_copies(
             t, ac.at[pad : 2 * pad, part], ac.at[frames : frames + pad, part], ac.at[:, part]
         )
         a_prev += to_prev
         a_next += to_next
-    run(has_prev, a_prev[:1], "start")
-    run(has_next, a_next[:1], "start")
-
     step = 16 if own % 16 == 0 else own
-    ones = jnp.ones((8, cells), F32)
-
-    def back(q):
+
+    def back(q, lo, hi, begin):
         part = pl.ds(q * step, step)
 
         def body(r, sums):
@@ -270,45 +269,64 @@
                 bf[c, f, r + 1, part] = (bt * gp[f, r, part]).astype(BF16)
             return tuple(sums)
 
-        zero = jnp.zeros((step, cells), F32)
-        return lax.fori_loop(0, rows, body, (zero,) * ntap)
-
-    with jax.named_scope("back"):
-        sums = [back(q) for q in range(own // step)]
-
-    g_chan = chan_copies(1, bf.at[c, :, 1 : rows + 1], bf.at[c, :, 1 : rows + 1])
+        return lax.fori_loop(lo, hi, body, begin)
+
+    def weight(lo, hi):
+        shifted = [[], [], []]
+        right = [[], [], []]
+        for f in range(frames):
+            line = [row_of(xf, f, r) for r in range(lo, hi + 2)]
+            for r in range(lo, hi):
+                v = bf[c, f, r + 1].astype(F32)
+                shifted[0].append(from_right(v).astype(BF16))
+                shifted[1].append(v.astype(BF16))
+                shifted[2].append(from_left(v).astype(BF16))
+                for i in range(3):
+                    right[i].append(line[r - lo + i])
+        left = jnp.concatenate([jnp.concatenate(x, axis=1) for x in shifted], axis=0)
+        for i in range(3):
+            rb[i * 3 * own : (i + 1) * 3 * own, :full] += lax.dot_general(
+                left, jnp.concatenate(right[i], axis=1), (((1,), (1,)), ((), ())),
+                preferred_element_type=F32,
+            )
+
+    sums = [(jnp.zeros((step, cells), F32),) * ntap] * (own // step)
+    g_chan = []
     g_up = up_copies(1, bf.at[c, :, 1], bf.at[c, :, rows + 1])
     g_down = down_copies(1, bf.at[c, :, rows], bf.at[c, :, 0])
-    for copy in g_chan:
-        copy.start()
-    run(has_up, g_up, "start")
-    run(has_down, g_down, "start")
-
     base = 9 * own
-    for k in range(ntap):
-        whole = jnp.concatenate([piece[k] for piece in sums], axis=0)
-        line = lax.dot_general(ones, whole, (((1,), (1,)), ((), ())),
-                               precision=lax.Precision.HIGHEST, preferred_element_type=F32)
-        rb[base + k : base + k + 1, :own] = line[:1]
-
-    def weight(f, carry):
-        shifted = [[], [], []]
-        for r in range(rows):
-            v = bf[c, f, r + 1].astype(F32)
-            shifted[0].append(from_right(v).astype(BF16))
-            shifted[1].append(v.astype(BF16))
-            shifted[2].append(from_left(v).astype(BF16))
-        left = jnp.concatenate([jnp.concatenate(x, axis=1) for x in shifted], axis=0)
-        line = rows_of(xf, f)
-        for i in range(3):
-            right = jnp.concatenate(line[i : i + rows], axis=1)
-            rb[i * 3 * own : (i + 1) * 3 * own, :full] += lax.dot_general(
-                left, right, (((1,), (1,)), ((), ())), preferred_element_type=F32
+    for t, (lo, hi) in enumerate(parts):
+        with jax.named_scope("wait_c"):
+            run(has_next, c_prev[t : t + 1], "wait_recv")
+            run(has_prev, c_next[t : t + 1], "wait_recv")
+        final = t == len(parts) - 1
+        if final:
+            run(has_prev, a_prev[:1], "start")
+            run(has_next, a_next[:1], "start")
+        with jax.named_scope("back"):
+            sums = [back(q, lo, hi, sums[q]) for q in range(own // step)]
+        lines = bf.at[c, :, 1 + lo : 1 + hi]
+        sent = chan_copies(1 + t, lines, lines)
+        g_chan += sent
+        for copy in sent:
+            copy.start()
+        if t == 0:
+            run(has_up, g_up, "start")
+        if final:
+            run(has_down, g_down, "start")
+            whole = jnp.concatenate([sums[q][k] for k in range(ntap) for q in range(own // step)], axis=0)
+            high = whole.astype(BF16)
+            rest = whole - high.astype(F32)
+            middle = rest.astype(BF16)
+            low = (rest - middle.astype(F32)).astype(BF16)
+            line = lax.dot_general(
+                jnp.ones((16, 3 * cells), BF16), jnp.concatenate([high, middle, low], axis=1),
+                (((1,), (1,)), ((), ())), preferred_element_type=F32,
             )
-        return carry
-
-    with jax.named_scope("wgt"):
-        lax.fori_loop(0, frames, weight, 0)
+            for k in range(ntap):
+                rb[base + k : base + k + 1, :own] = line[:1, k * own : (k + 1) * own]
+        with jax.named_scope("wgt"):
+            weight(lo, hi)
 
     def scatter(d):
         other, device = peer(d)
@@ -370,7 +388,7 @@
         return carry
 
     with jax.named_scope("bwd"):
-        lax.fori_loop(0, frames, backward, 0)
+        lax.fori_loop(0, frames, backward, 0, unroll=True)
 
     with jax.named_scope("wait_rs"):
         each(scatter, "wait_recv")
@@ -427,6 +445,13 @@
     run(has_next, c_next + a_next, "wait_send")
     each(scatter, "wait_send")
     each(gather, "wait_send")
+
+
+def row_parts(rows):
+    first = max(rows // 2, 1)
+    second = first + max((rows - first) // 2, 0)
+    cuts = sorted({0, first, second, rows})
+    return list(zip(cuts[:-1], cuts[1:]))
 
 
 def ship(*refs):
@@ -458,6 +483,7 @@
     scale = float(frames * nh * rows * ns * cells) ** (-0.5)
     vmem = pl.BlockSpec(memory_space=pltpu.VMEM)
     dma = pltpu.SemaphoreType.DMA
+    count = len(row_parts(rows))
     limit = 20 * 2**20 if rows * frames <= 16 else 56 * 2**20
     hbm = pl.BlockSpec(memory_space=pltpu.HBM)
     shapes = (
@@ -490,12 +516,12 @@
             pltpu.VMEM(time_weight.shape, BF16),
             pltpu.SemaphoreType.REGULAR((max(nh + ns - 3, 1),)),
             dma((4,)),
-            dma((2, nc - 1)),
-            dma((2, nc - 1)),
+            dma((count + 1, nc - 1)),
+            dma((count + 1, nc - 1)),
             dma((2, 2, nc)),
             dma((2, 2, nc)),
-            dma((3, 2)),
-            dma((3, 2)),
+            dma((count + 2, 2)),
+            dma((count + 2, 2)),
             dma((2, n - 1)),
             dma((2, n - 1)),
         ],

time: 24.8 us -> 24.9 us (level)
  no operation moved by 1% of the time
where the time goes in v4:
time: 24.9 us; the launch traced here: 24.7 us
  Pallas kernels  24.1 us (97%)
  between operations  0.64 us (3%)
    pallas_call x1, Pallas kernels, on_device(): pl.pallas_call(functools.partial(block, (nh, ns, nc, scale), (spare, piec...  23.2 us
    pallas_call x1, Pallas kernels, on_device(): pl.pallas_call(ship, out_shape=tuple((jax.ShapeDtypeStruct(*x) for x in s...  0.85 us

profile of v4, /device:TPU:0, one launch (start us, length us, event | category | flops | bytes accessed | tf_op | source)
XLA Modules:
  0.0 24.7 jit_solution(1558982513090571239)
XLA Ops:
  0.6 23.2 %shard_map.75 = (bf16[4,4,48,128]{3,2,1,0:T(8,128)(2,1)S(1)}, bf16[4,4,48,128]{3,2,1,0:T(8,128)(2,1)S(1)}, f32[3,3,48,96]{3,2,1,0:T(8,128)S(1)}, f32[9,48]{1,0:T(8,128)S(1)}) custom-call(bf16[4,4,48,128]{3,2,1,0:T(8,128)(2,1)} %field.1, bf16[4,4,48,128]{3,2,1,0:T(8,128)(2,1)} %cot.1, bf16[3,3,96,96]{3,2,1,0:T(8,128)(2,1)} %sw.1, bf16[9,48]{1,0:T(8,128)(2,1)} %tw.1), custom_call_target="tpu_custom_call" | custom-call | tf_op jit(solution)/shard_map/pallas_call | solution.py:495
  23.9 0.9 %shard_map.76 = (bf16[4,4,48,128]{3,2,1,0:T(8,128)(2,1)}, bf16[4,4,48,128]{3,2,1,0:T(8,128)(2,1)}, f32[3,3,48,96]{3,2,1,0:T(8,128)}, f32[9,48]{1,0:T(8,128)}) custom-call(bf16[4,4,48,128]{3,2,1,0:T(8,128)(2,1)S(1)} %get-tuple-element.8.refs_0_, bf16[4,4,48,128]{3,2,1,0:T(8,128)(2,1)S(1)} %get-tuple-element.9.refs_1_, ...), custom_call_target="tpu_custom_call" | custom-call | tf_op jit(solution)/shard_map/pallas_call | solution.py:532

commit v5 on v4

--- a/solution.py
+++ b/solution.py
@@ -240,15 +240,16 @@
     with jax.named_scope("fwd"):
         lax.fori_loop(0, frames, forward, 0, unroll=True)
 
-    heard(1)
-    half = max(rows // 2, 1)
     a_prev, a_next = [], []
-    for t, part in ((len(parts), slice(0, half)), (len(parts) + 1, slice(half, rows))):
+    for t, (lo, hi) in enumerate(parts):
+        part = slice(lo, hi)
         to_prev, to_next = time_copies(
-            t, ac.at[pad : 2 * pad, part], ac.at[frames : frames + pad, part], ac.at[:, part]
+            len(parts) + t, ac.at[pad : 2 * pad, part], ac.at[frames : frames + pad, part], ac.at[:, part]
         )
         a_prev += to_prev
         a_next += to_next
+    run(has_prev, a_prev[:1], "start")
+    run(has_next, a_next[:1], "start")
     step = 16 if own % 16 == 0 else own
 
     def back(q, lo, hi, begin):
@@ -301,8 +302,8 @@
             run(has_prev, c_next[t : t + 1], "wait_recv")
         final = t == len(parts) - 1
         if final:
-            run(has_prev, a_prev[:1], "start")
-            run(has_next, a_next[:1], "start")
+            run(has_prev, a_prev[1:2], "start")
+            run(has_next, a_next[1:2], "start")
         with jax.named_scope("back"):
             sums = [back(q, lo, hi, sums[q]) for q in range(own // step)]
         lines = bf.at[c, :, 1 + lo : 1 + hi]
@@ -362,11 +363,11 @@
             rbb[t * extra : (t + 1) * extra] = mixed.astype(BF16)
     else:
         rbb[:packed] = rb[...].astype(BF16)
-    for t in range(2, rounds):
+    for t in range(1, rounds):
         heard(t)
     each(scatter, "start")
-    run(has_prev, a_prev[1:], "start")
-    run(has_next, a_next[1:], "start")
+    run(has_prev, a_prev[2:], "start")
+    run(has_next, a_next[2:], "start")
 
     with jax.named_scope("wait_g"):
         for copy in g_chan:
@@ -520,8 +521,8 @@
             dma((count + 1, nc - 1)),
             dma((2, 2, nc)),
             dma((2, 2, nc)),
-            dma((count + 2, 2)),
-            dma((count + 2, 2)),
+            dma((2 * count, 2)),
+            dma((2 * count, 2)),
             dma((2, n - 1)),
             dma((2, n - 1)),
         ],

time: 24.9 us -> 24.2 us (0.972)
  Pallas kernels: 24.1 us -> 23.4 us
    pallas_call x1, Pallas kernels: 23.2 us -> 22.5 us  [on_device(): pl.pallas_call(functools.partial(block, (nh, ns, nc, scale), (spare, piec...]
where the time goes in v5:
time: 24.2 us; the launch traced here: 24 us
  Pallas kernels  23.4 us (97%)
  between operations  0.64 us (3%)
    pallas_call x1, Pallas kernels, on_device(): pl.pallas_call(functools.partial(block, (nh, ns, nc, scale), (spare, piec...  22.5 us
    pallas_call x1, Pallas kernels, on_device(): pl.pallas_call(ship, out_shape=tuple((jax.ShapeDtypeStruct(*x) for x in s...  0.85 us

profile of v5, /device:TPU:0, one launch (start us, length us, event | category | flops | bytes accessed | tf_op | source)
XLA Modules:
  0.0 24.0 jit_solution(14643636070197816036)
XLA Ops:
  0.6 22.5 %shard_map.75 = (bf16[4,4,48,128]{3,2,1,0:T(8,128)(2,1)S(1)}, bf16[4,4,48,128]{3,2,1,0:T(8,128)(2,1)S(1)}, f32[3,3,48,96]{3,2,1,0:T(8,128)S(1)}, f32[9,48]{1,0:T(8,128)S(1)}) custom-call(bf16[4,4,48,128]{3,2,1,0:T(8,128)(2,1)} %field.1, bf16[4,4,48,128]{3,2,1,0:T(8,128)(2,1)} %cot.1, bf16[3,3,96,96]{3,2,1,0:T(8,128)(2,1)} %sw.1, bf16[9,48]{1,0:T(8,128)(2,1)} %tw.1), custom_call_target="tpu_custom_call" | custom-call | tf_op jit(solution)/shard_map/pallas_call | solution.py:496
  23.2 0.9 %shard_map.76 = (bf16[4,4,48,128]{3,2,1,0:T(8,128)(2,1)}, bf16[4,4,48,128]{3,2,1,0:T(8,128)(2,1)}, f32[3,3,48,96]{3,2,1,0:T(8,128)}, f32[9,48]{1,0:T(8,128)}) custom-call(bf16[4,4,48,128]{3,2,1,0:T(8,128)(2,1)S(1)} %get-tuple-element.8.refs_0_, bf16[4,4,48,128]{3,2,1,0:T(8,128)(2,1)S(1)} %get-tuple-element.9.refs_1_, ...), custom_call_target="tpu_custom_call" | custom-call | tf_op jit(solution)/shard_map/pallas_call | solution.py:533
